TPU v7x, 32 devices: a whole 2x2x4 slice. The times are simulated.
32 devices in a mesh: row: 2 (over y), pair: 16 (over z, x, core).
Axes of the slice: x: 2, y: 2, z: 4, core: 2. Of those that a mesh axis runs over, the one named last changes fastest.
Arguments:
- panel: float32 [4096, 4096], P('row', 'pair'), may hold values from -51 to 51
- slot_block: int32 [32], replicated, may hold values from 0 to 31, each once
Outputs:
- rotated: float32 [4096, 4096], P('row', 'pair')
Inputs may be any that keep to these rules, and one draw needn't show every extreme that they name: `slot_block`: each block number appears once.
All inputs are finite; a program needn't handle non-finite values.
Results may differ from a plain program's by a relative error of at most 0.0003.
Values sent between devices are 32-bit elements; how exact they have to be, the bound alone decides.
A program may use at most 64 MiB of HBM per device.

v0:
```python
import jax
import jax.numpy as jnp
from jax import lax
from jax.sharding import PartitionSpec as P

STEPS = 2
NS_ITERS = 3
precise = lax.Precision.HIGHEST


def passed_along(value, axis, steps):
    count = lax.axis_size(axis)
    initial, last = (max(0, -steps), min(count, count - steps))
    return lax.ppermute(value, axis, [(source, source + steps) for source in range(initial, last)])


def inverse_root(matrix):
    identity = jnp.eye(matrix.shape[0], dtype=matrix.dtype)
    approx = matrix
    root_inv = identity
    for sweep in range(NS_ITERS):
        factor = 1.5 * identity - 0.5 * jnp.dot(root_inv, approx, precision=precise)
        approx = jnp.dot(approx, factor, precision=precise)
        root_inv = jnp.dot(factor, root_inv, precision=precise)
    return root_inv / jnp.sqrt(5.0)


def couple(cross):
    identity = jnp.eye(cross.shape[0], dtype=cross.dtype)
    coupling = cross * (2.0 / jnp.sqrt(jnp.sum(cross * cross) + 1e-06))
    left = (identity + jnp.dot(coupling, coupling.T, precision=precise)) / 5.0
    right = (identity + jnp.dot(coupling.T, coupling, precision=precise)) / 5.0
    return (coupling, left, right)


def inner_rows(first, second):
    return lax.dot_general(first, second, (((0,), (0,)), ((), ())), precision=precise)


def move_slots(uppers, lowers):
    new_uppers = jnp.concatenate([uppers[0:1], lowers[0:1], uppers[1:-1]], axis=0)
    new_lowers = jnp.concatenate([lowers[1:], uppers[-1:]], axis=0)
    return (new_uppers, new_lowers)


def jacobi_step(upper, lower, upper_ids, lower_ids, position, pairs):
    matching = jnp.arange(pairs) == position
    upper_id = jnp.sum(jnp.where(matching, upper_ids, 0))
    lower_id = jnp.sum(jnp.where(matching, lower_ids, 0))
    order_flag = upper_id < lower_id
    first = jnp.where(order_flag, upper, lower)
    second = jnp.where(order_flag, lower, upper)
    cross = lax.psum(inner_rows(first, second), "row")
    coupling, left, right = couple(cross)
    left_inverse = inverse_root(left)
    right_inverse = inverse_root(right)
    new_first = jnp.dot(
        first + jnp.dot(second, coupling.T, precision=precise), left_inverse, precision=precise
    )
    new_second = jnp.dot(
        second - jnp.dot(first, coupling, precision=precise), right_inverse, precision=precise
    )
    new_upper = jnp.where(order_flag, new_first, new_second)
    new_lower = jnp.where(order_flag, new_second, new_first)
    carried = jnp.where(position == 0, new_lower, new_upper)
    from_left = passed_along(carried, "pair", 1)
    from_right = passed_along(new_lower, "pair", -1)
    moved_upper = jnp.where(position == 0, new_upper, from_left)
    moved_lower = jnp.where(position == pairs - 1, new_upper, from_right)
    return (moved_upper, moved_lower)


def per_device(panel, slot_block):
    width = panel.shape[1] // 2
    pairs = lax.axis_size("pair")
    position = lax.axis_index("pair")
    upper = panel[:, :width]
    lower = panel[:, width:]
    upper_ids = slot_block[:pairs]
    lower_ids = slot_block[pairs:]
    for step in range(STEPS):
        upper, lower = jacobi_step(upper, lower, upper_ids, lower_ids, position, pairs)
        upper_ids, lower_ids = move_slots(upper_ids, lower_ids)
    return jnp.concatenate([upper, lower], axis=1)


def solution(mesh):
    in_specs = (P("row", "pair"), P())
    out_specs = P("row", "pair")
    return jax.shard_map(
        per_device, mesh=mesh, in_specs=in_specs, out_specs=out_specs, check_vma=False
    )
```

profile of v0, /device:TPU:9, one launch (start us, length us, event | category | flops | bytes accessed | tf_op | source)
XLA Modules:
  0.0 150.3 jit_solution(13770389145376605013)
XLA Ops:
  6.5 1.5 %select_reduce_fusion = (s32[]{:T(128)}, s32[]{:T(128)}) fusion(s32[32]{0:T(128)} %param.3, s32[]{:T(128)S(6)} %axis_index.12), kind=kLoop, calls=%fused_computation.82 | loop fusion | flops 78 | bytes 140 | tf_op jit(solution)/shard_map/reduce_sum | solution.py:49
  9.4 1.7 %slice_select_fusion.1 = (f32[2048,128]{1,0:T(8,128)S(1)}, f32[2048,128]{1,0:T(8,128)S(1)}) fusion(f32[2048,256]{1,0:T(8,128)} %param.2, pred[]{:T(512)S(6)} %lt.7), kind=kLoop, calls=%fused_computation.42 | loop fusion | flops 524288 | bytes 4194305 | tf_op jit(solution)/shard_map/jit(_where)/select_n | solution.py:51
  11.1 2.4 %fusion.39 = f32[128,128]{1,0:T(8,128)} fusion(f32[2048,128]{1,0:T(8,128)S(1)} %get-tuple-element.15, f32[2048,128]{1,0:T(8,128)S(1)} %get-tuple-element.16), kind=kOutput, calls=%fused_computation.86 | convolution fusion | flops 402653184 | bytes 2162688 | tf_op jit(solution)/shard_map/dot_general | solution.py:37
  13.6 21.8 %all-reduce.3.cloned.1.call-done = f32[128,128]{1,0:T(8,128)} async-done(((f32[128,128]{1,0:T(8,128)}), f32[128,128]{1,0:T(8,128)}) %all-reduce.3.cloned.1.call-update) | async-done | bytes 65552 | tf_op jit(solution)/shard_map/psum | solution.py:53
  35.4 1.5 %multiply_reduce_fusion.1 = f32[]{:T(128)} fusion(f32[128,128]{1,0:T(8,128)} %all-reduce.3.cloned.1.call-done), kind=kLoop, calls=%fused_computation.61 | loop fusion | flops 32767 | bytes 65540 | tf_op jit(solution)/shard_map/reduce_sum | solution.py:30
  37.6 1.2 fusion.11
  40.0 1.2 fusion.15
  43.3 1.0 convolution_add_fusion.1
  44.3 1.0 fusion.43
  45.3 1.0 convolution_subtract_fusion.1
  46.3 2.0 %broadcast_select_fusion.11 = (f32[2048,128]{1,0:T(8,128)}, f32[2048,128]{1,0:T(8,128)S(1)}, f32[2048,128]{1,0:T(8,128)S(1)}) fusion(pred[]{:T(512)S(6)} %eq.72, f32[2048,128]{1,0:T(8,128)S(1)} %fusion.43, pred[]{:T(512)S(6)} %lt.7, f32[2048,128]{1,0:T(8,128)S(1)} %convolution_subtract_fusion.1, f32[128,128]{1,0:T(8,128)S(1)} %convolution_multiply_fusion.8), kind=kOutput, calls=%fused_computation.54 | convolution fusion | flops 403439616 | bytes 5308418 | tf_op jit(solution)/shard_map/dot_general | solution.py:60
  48.3 4.1 %collective-permute-start = (f32[2048,128]{1,0:T(8,128)}, f32[2048,128]{1,0:T(8,128)S(1)}, u32[]{:S(2)}, u32[]{:S(2)}) collective-permute-start(f32[2048,128]{1,0:T(8,128)} %get-tuple-element.10), channel_id=1, source_target_pairs={{0,1},{1,2},{2,3},{3,4},{4,5},{5,6},{6,7},{7,8},{8,9},{9,10},{10,1... | collective-permute-start | bytes 3145736 | tf_op jit(solution)/shard_map/ppermute | solution.py:14
  52.4 2.1 %collective-permute-start.1 = (f32[2048,128]{1,0:T(8,128)S(1)}, f32[2048,128]{1,0:T(8,128)}, u32[]{:S(2)}, u32[]{:S(2)}) collective-permute-start(f32[2048,128]{1,0:T(8,128)S(1)} %get-tuple-element.11), channel_id=1, source_target_pairs={{1,0},{2,1},{3,2},{4,3},{5,4},{6,5},{7,6},{8,7},{9,8},{10,9},{11,1... | collective-permute-start | bytes 3145736 | tf_op jit(solution)/shard_map/ppermute | solution.py:14
  54.6 0.7 fusion.38
  55.3 2.6 %fusion.36 = (s32[]{:T(128)}, s32[]{:T(128)}) fusion(s32[14]{0:T(128)S(1)} %slice.34, s32[1]{0:T(128)} %get-tuple-element.20, s32[1]{0:T(128)} %get-tuple-element.21, s32[]{:T(128)S(6)} %axis_index.12, s32[1]{0:T(128)} %get-tuple-element.19, s32[15]{0:T(128)S(1)} %slice.35), kind=kLoop, calls=%fused_computation.79 | loop fusion | flops 126 | bytes 140 | tf_op jit(solution)/shard_map/reduce_sum | solution.py:48
  59.2 16.5 %collective-permute-done = f32[2048,128]{1,0:T(8,128)S(1)} collective-permute-done((f32[2048,128]{1,0:T(8,128)}, f32[2048,128]{1,0:T(8,128)S(1)}, u32[]{:S(2)}, u32[]{:S(2)}) %collective-permute-start) | collective-permute-done | bytes 1048608 | tf_op jit(solution)/shard_map/ppermute | solution.py:14
  75.7 1.6 %collective-permute-done.1 = f32[2048,128]{1,0:T(8,128)} collective-permute-done((f32[2048,128]{1,0:T(8,128)S(1)}, f32[2048,128]{1,0:T(8,128)}, u32[]{:S(2)}, u32[]{:S(2)}) %collective-permute-start.1) | collective-permute-done | bytes 1048608 | tf_op jit(solution)/shard_map/ppermute | solution.py:14
  77.3 1.7 %broadcast_select_fusion.7 = (f32[2048,128]{1,0:T(8,128)S(1)}, f32[2048,128]{1,0:T(8,128)S(1)}) fusion(pred[]{:T(512)S(6)} %lt.6, f32[2048,128]{1,0:T(8,128)S(1)} %get-tuple-element.12, f32[2048,128]{1,0:T(8,128)} %copy-done.2, pred[]{:T(512)S(6)} %eq.72, f32[2048,128]{1,0:T(8,128)} %collective-permute-done.1, pred[]{:T(512)S(6)} %eq.76), kind=kLoop, calls=%fused_computation.50 | loop fusion | flops 1048576 | bytes 5242883 | tf_op jit(solution)/shard_map/jit(_where)/select_n | solution.py:51
  79.0 2.4 %fusion.47 = f32[128,128]{1,0:T(8,128)} fusion(f32[2048,128]{1,0:T(8,128)S(1)} %get-tuple-element.13, f32[2048,128]{1,0:T(8,128)S(1)} %get-tuple-element.14), kind=kOutput, calls=%fused_computation.94 | convolution fusion | flops 402653184 | bytes 2162688 | tf_op jit(solution)/shard_map/dot_general | solution.py:37
  81.5 19.7 %all-reduce.5.cloned.1.call-done = f32[128,128]{1,0:T(8,128)} async-done(((f32[128,128]{1,0:T(8,128)}), f32[128,128]{1,0:T(8,128)}) %all-reduce.5.cloned.1.call-update) | async-done | bytes 65552 | tf_op jit(solution)/shard_map/psum | solution.py:53
  101.2 1.5 %multiply_reduce_fusion = f32[]{:T(128)} fusion(f32[128,128]{1,0:T(8,128)} %all-reduce.5.cloned.1.call-done), kind=kLoop, calls=%fused_computation.55 | loop fusion | flops 32767 | bytes 65540 | tf_op jit(solution)/shard_map/reduce_sum | solution.py:30
  103.4 1.2 fusion.3
  105.8 1.2 fusion.7
  109.1 1.0 convolution_add_fusion
  110.1 1.0 fusion.51
  111.1 1.0 convolution_subtract_fusion
  112.1 1.0 broadcast_select_fusion.9
  113.1 4.1 %collective-permute-start.2 = (f32[2048,128]{1,0:T(8,128)S(1)}, f32[2048,128]{1,0:T(8,128)S(1)}, u32[]{:S(2)}, u32[]{:S(2)}) collective-permute-start(f32[2048,128]{1,0:T(8,128)S(1)} %get-tuple-element.7), channel_id=1, source_target_pairs={{0,1},{1,2},{2,3},{3,4},{4,5},{5,6},{6,7},{7,8},{8,9},{9,10},{10,1... | collective-permute-start | bytes 3145736 | tf_op jit(solution)/shard_map/ppermute | solution.py:14
  117.2 1.9 %collective-permute-start.3 = (f32[2048,128]{1,0:T(8,128)S(1)}, f32[2048,128]{1,0:T(8,128)S(1)}, u32[]{:S(2)}, u32[]{:S(2)}) collective-permute-start(f32[2048,128]{1,0:T(8,128)S(1)} %get-tuple-element.8), channel_id=1, source_target_pairs={{1,0},{2,1},{3,2},{4,3},{5,4},{6,5},{7,6},{8,7},{9,8},{10,9},{11,1... | collective-permute-start | bytes 3145736 | tf_op jit(solution)/shard_map/ppermute | solution.py:14
  119.1 21.0 %collective-permute-done.2 = f32[2048,128]{1,0:T(8,128)S(1)} collective-permute-done((f32[2048,128]{1,0:T(8,128)S(1)}, f32[2048,128]{1,0:T(8,128)S(1)}, u32[]{:S(2)}, u32[]{:S(2)}) %collective-permute-start.2) | collective-permute-done | bytes 1048608 | tf_op jit(solution)/shard_map/ppermute | solution.py:14
  140.2 1.6 %collective-permute-done.3 = f32[2048,128]{1,0:T(8,128)S(1)} collective-permute-done((f32[2048,128]{1,0:T(8,128)S(1)}, f32[2048,128]{1,0:T(8,128)S(1)}, u32[]{:S(2)}, u32[]{:S(2)}) %collective-permute-start.3) | collective-permute-done | bytes 1048608 | tf_op jit(solution)/shard_map/ppermute | solution.py:14
  142.0 1.5 pad_maximum_fusion
  (47 shorter events, 6.8 us)
Async XLA Ops:
  6.5 28.8 %all-reduce.3.cloned.1.call-start = ((), (), s32[]{:S(2)}) async-start(), calls=%async_computation | async-start | bytes 131072 | tf_op jit(solution)/shard_map/psum | solution.py:53
  13.6 87.6 %all-reduce.5.cloned.1.call-start = ((), (), s32[]{:S(2)}) async-start(), calls=%async_computation.1 | async-start | bytes 131072 | tf_op jit(solution)/shard_map/psum | solution.py:53
  35.4 7.9 %copy-start = (f32[128,128]{1,0:T(8,128)S(1)}, f32[128,128]{1,0:T(8,128)}, u32[]{:S(2)}) copy-start(f32[128,128]{1,0:T(8,128)} %all-reduce.3.cloned.1.call-done) | copy-start | bytes 196612
  46.3 8.2 %copy-start.3 = (s32[32]{0:T(128)S(1)}, s32[32]{0:T(128)}, u32[]{:S(2)}) copy-start(s32[32]{0:T(128)} %param.3) | copy-start | bytes 388
  48.3 27.4 %collective-permute-start = (f32[2048,128]{1,0:T(8,128)}, f32[2048,128]{1,0:T(8,128)S(1)}, u32[]{:S(2)}, u32[]{:S(2)}) collective-permute-start(f32[2048,128]{1,0:T(8,128)} %get-tuple-element.10), channel_id=1, source_target_pairs={{0,1},{1,2},{2,3},{3,4},{4,5},{5,6},{6,7},{7,8},{8,9},{9,10},{10,1... | collective-permute-start | bytes 3145736 | tf_op jit(solution)/shard_map/ppermute | solution.py:14
  52.4 24.9 %collective-permute-start.1 = (f32[2048,128]{1,0:T(8,128)S(1)}, f32[2048,128]{1,0:T(8,128)}, u32[]{:S(2)}, u32[]{:S(2)}) collective-permute-start(f32[2048,128]{1,0:T(8,128)S(1)} %get-tuple-element.11), channel_id=1, source_target_pairs={{1,0},{2,1},{3,2},{4,3},{5,4},{6,5},{7,6},{8,7},{9,8},{10,9},{11,1... | collective-permute-start | bytes 3145736 | tf_op jit(solution)/shard_map/ppermute | solution.py:14
  75.7 1.6 %copy-start.2 = (f32[2048,128]{1,0:T(8,128)}, f32[2048,128]{1,0:T(8,128)S(1)}, u32[]{:S(2)}) copy-start(f32[2048,128]{1,0:T(8,128)S(1)} %collective-permute-done) | copy-start | bytes 3145732
  101.2 7.9 %copy-start.1 = (f32[128,128]{1,0:T(8,128)S(1)}, f32[128,128]{1,0:T(8,128)}, u32[]{:S(2)}) copy-start(f32[128,128]{1,0:T(8,128)} %all-reduce.5.cloned.1.call-done) | copy-start | bytes 196612
  113.1 27.1 %collective-permute-start.2 = (f32[2048,128]{1,0:T(8,128)S(1)}, f32[2048,128]{1,0:T(8,128)S(1)}, u32[]{:S(2)}, u32[]{:S(2)}) collective-permute-start(f32[2048,128]{1,0:T(8,128)S(1)} %get-tuple-element.7), channel_id=1, source_target_pairs={{0,1},{1,2},{2,3},{3,4},{4,5},{5,6},{6,7},{7,8},{8,9},{9,10},{10,1... | collective-permute-start | bytes 3145736 | tf_op jit(solution)/shard_map/ppermute | solution.py:14
  117.2 24.6 %collective-permute-start.3 = (f32[2048,128]{1,0:T(8,128)S(1)}, f32[2048,128]{1,0:T(8,128)S(1)}, u32[]{:S(2)}, u32[]{:S(2)}) collective-permute-start(f32[2048,128]{1,0:T(8,128)S(1)} %get-tuple-element.8), channel_id=1, source_target_pairs={{1,0},{2,1},{3,2},{4,3},{5,4},{6,5},{7,6},{8,7},{9,8},{10,9},{11,1... | collective-permute-start | bytes 3145736 | tf_op jit(solution)/shard_map/ppermute | solution.py:14
Sparse Core Ops, SparseCore 0:
  13.7 21.6 all-reduce.2
  81.6 19.5 all-reduce.4
where the time goes:
time: 151 us; the launch traced here: 150 us
  waiting for transfers between devices  82.3 us (55%)
  matrix products  24.9 us (16%)
  between operations  17.7 us (12%)
  starting transfers between devices  12.3 us (8%)
  other arithmetic  12.3 us (8%)
    psum x2, waiting for transfers between devices, jacobi_step(): cross = lax.psum(inner_rows(first, second), 'row')  41.5 us
    ppermute x4, waiting for transfers between devices, passed_along(): lax.ppermute(value, axis, [(source, source + steps) for source in range(i...  40.7 us
    ppermute x4, starting transfers between devices, passed_along(): lax.ppermute(value, axis, [(source, source + steps) for source in range(i...  12.2 us
    dot_general x2, matrix products, inner_rows(): lax.dot_general(first, second, (((0,), (0,)), ((), ())), precision=precise)  4.89 us
    select_n x2, other arithmetic, jacobi_step(): first = jnp.where(order_flag, upper, lower)  3.41 us
    reduce_sum x2, other arithmetic, couple(): coupling = cross * (2.0 / jnp.sqrt(jnp.sum(cross * cross) + 1e-06))  3.06 us
  transfers between devices with their start and end apart: 6, of which 6 were waited for; matrix products, arithmetic and copies ran while one was open for 2% of the time, Pallas kernels for 0%

commit v1 on v0

--- a/solution.py
+++ b/solution.py
@@ -1,3 +1,4 @@
+import functools
 import jax
 import jax.numpy as jnp
 from jax import lax
@@ -6,6 +7,13 @@
 STEPS = 2
 NS_ITERS = 3
 precise = lax.Precision.HIGHEST
+
+
+def play_samples_all(own_rows, net_axis):
+    return lax.all_gather(own_rows, net_axis).sum(axis=0)
+
+
+joints_post = functools.partial(play_samples_all, net_axis="row")
 
 
 def passed_along(value, axis, steps):
@@ -50,7 +58,7 @@
     order_flag = upper_id < lower_id
     first = jnp.where(order_flag, upper, lower)
     second = jnp.where(order_flag, lower, upper)
-    cross = lax.psum(inner_rows(first, second), "row")
+    cross = joints_post(inner_rows(first, second))
     coupling, left, right = couple(cross)
     left_inverse = inverse_root(left)
     right_inverse = inverse_root(right)

time: 151 us -> 99.5 us (0.66)
  waiting for transfers between devices: 82.3 us -> 39.5 us
  between operations: 17.7 us -> 4.36 us
  blocking collectives: 0 us -> 7.74 us
  matrix products: 24.9 us -> 21.2 us
  other arithmetic: 12.3 us -> 10.4 us
    psum x2 -> x0, waiting for transfers between devices: 41.5 us -> none  [jacobi_step(): cross = lax.psum(inner_rows(first, second), 'row')]
    all_gather x0 -> x2, blocking collectives: none -> 7.74 us  [play_samples_all(): return lax.all_gather(own_rows, net_axis).sum(axis=0)]
    reduce_sum x2, other arithmetic: 3.06 us -> 1.23 us  [couple(): coupling = cross * (2.0 / jnp.sqrt(jnp.sum(cross * cross) + 1e-06))]
    dot_general x2, matrix products: 2.37 us -> 0.54 us  [couple(): left = (identity + jnp.dot(coupling, coupling.T, precision=precise)) / 5.0]
    dot_general x2, matrix products: 2.4 us -> 0.57 us  [couple(): right = (identity + jnp.dot(coupling.T, coupling, precision=precise)) / 5.0]
  transfers between devices with their start and end apart: 6 -> 4, of which waited for: 6 -> 3; matrix products, arithmetic and copies ran while one was open for 2% -> 4% of each run, Pallas kernels for 0% -> 0%
where the time goes in v1:
time: 99.5 us; the launch traced here: 98.3 us
  waiting for transfers between devices  39.5 us (40%)
  matrix products  21.2 us (21%)
  starting transfers between devices  13.3 us (13%)
  other arithmetic  10.4 us (10%)
  blocking collectives  7.74 us (8%)
  between operations  4.36 us (4%)
  local copies, waits for them, and re-layouts  1.82 us (2%)
    ppermute x4, waiting for transfers between devices, passed_along(): lax.ppermute(value, axis, [(source, source + steps) for source in range(i...  39.5 us
    ppermute x4, starting transfers between devices, passed_along(): lax.ppermute(value, axis, [(source, source + steps) for source in range(i...  13.3 us
    all_gather x2, blocking collectives, play_samples_all(): return lax.all_gather(own_rows, net_axis).sum(axis=0)  7.74 us
    dot_general x2, matrix products, inner_rows(): lax.dot_general(first, second, (((0,), (0,)), ((), ())), precision=precise)  3.63 us
    select_n x2, other arithmetic, jacobi_step(): first = jnp.where(order_flag, upper, lower)  3.4 us
    dot_general x2, matrix products, jacobi_step(): jnp.dot(second - jnp.dot(first, coupling, precision=precise), right_inver...  3.28 us
    dot_general x2, matrix products, jacobi_step(): jnp.dot(first, coupling, precision=precise)  2.93 us
    reduce_sum x1, other arithmetic, jacobi_step(): upper_id = jnp.sum(jnp.where(matching, upper_ids, 0))  2.65 us
  transfers between devices with their start and end apart: 4, of which 3 were waited for; matrix products, arithmetic and copies ran while one was open for 4% of the time, Pallas kernels for 0%

profile of v1, /device:TPU:9, one launch (start us, length us, event | category | flops | bytes accessed | tf_op | source)
XLA Modules:
  0.0 98.3 jit_solution(14807327015197611483)
XLA Ops:
  0.0 1.5 %select_reduce_fusion = (s32[]{:T(128)}, s32[]{:T(128)}) fusion(s32[32]{0:T(128)} %param.3, s32[]{:T(128)S(6)} %axis_index.12), kind=kLoop, calls=%fused_computation.82 | loop fusion | flops 78 | bytes 140 | tf_op jit(solution)/shard_map/reduce_sum | solution.py:57
  2.9 1.7 %slice_select_fusion.1 = (f32[2048,128]{1,0:T(8,128)S(1)}, f32[2048,128]{1,0:T(8,128)S(1)}) fusion(f32[2048,256]{1,0:T(8,128)} %param.2, pred[]{:T(512)S(6)} %lt.7), kind=kLoop, calls=%fused_computation.42 | loop fusion | flops 524288 | bytes 4194305 | tf_op jit(solution)/shard_map/jit(_where)/select_n | solution.py:59
  4.5 1.8 %fusion.39 = f32[128,128]{1,0:T(8,128)S(1)} fusion(f32[2048,128]{1,0:T(8,128)S(1)} %get-tuple-element.15, f32[2048,128]{1,0:T(8,128)S(1)} %get-tuple-element.16), kind=kOutput, calls=%fused_computation.86 | convolution fusion | flops 402653184 | bytes 2162688 | tf_op jit(solution)/shard_map/dot_general | solution.py:45
  6.4 3.8 %all-gather = f32[256,128]{1,0:T(8,128)S(1)} all-gather(f32[128,128]{1,0:T(8,128)S(1)} %fusion.39), channel_id=2, replica_groups=mesh['row'=2,'pair'=16] {'row'}, dimensions={0}, use_global_device_ids=true | all-gather | bytes 196608 | tf_op jit(solution)/shard_map/all_gather | solution.py:13
  10.2 0.6 multiply_reduce_fusion.1
  11.5 0.3 fusion.11
  13.0 0.3 fusion.15
  14.5 1.9 %convolution_subtract_fusion.1 = f32[2048,128]{1,0:T(8,128)} fusion(f32[2048,128]{1,0:T(8,128)S(1)} %get-tuple-element.16, f32[2048,128]{1,0:T(8,128)S(1)} %get-tuple-element.15, f32[128,128]{1,0:T(8,128)S(1)} %reduce_sum.76, f32[]{:T(128)S(6)} %div.30), kind=kOutput, calls=%fused_computation.2 | convolution fusion | flops 402931712 | bytes 3211268 | tf_op jit(solution)/shard_map/dot_general | solution.py:69
  16.4 1.0 %convolution_add_fusion.1 = f32[2048,128]{1,0:T(8,128)S(1)} fusion(f32[2048,128]{1,0:T(8,128)S(1)} %get-tuple-element.15, f32[2048,128]{1,0:T(8,128)S(1)} %get-tuple-element.16, f32[128,128]{1,0:T(8,128)S(1)} %reduce_sum.76, f32[]{:T(128)S(6)} %div.30), kind=kOutput, calls=%fused_computation.3 | convolution fusion | flops 402931712 | bytes 3211268 | tf_op jit(solution)/shard_map/dot_general | solution.py:66
  18.3 1.0 fusion.43
  19.3 2.3 %broadcast_select_fusion.11 = (f32[2048,128]{1,0:T(8,128)}, f32[2048,128]{1,0:T(8,128)}, f32[2048,128]{1,0:T(8,128)S(1)}) fusion(pred[]{:T(512)S(6)} %eq.72, f32[2048,128]{1,0:T(8,128)S(1)} %fusion.43, pred[]{:T(512)S(6)} %lt.7, f32[2048,128]{1,0:T(8,128)S(1)} %copy-done, f32[128,128]{1,0:T(8,128)S(1)} %convolution_multiply_fusion.8), kind=kOutput, calls=%fused_computation.54 | convolution fusion | flops 403439616 | bytes 5308418 | tf_op jit(solution)/shard_map/dot_general | solution.py:68
  21.6 4.8 %collective-permute-start = (f32[2048,128]{1,0:T(8,128)}, f32[2048,128]{1,0:T(8,128)S(1)}, u32[]{:S(2)}, u32[]{:S(2)}) collective-permute-start(f32[2048,128]{1,0:T(8,128)} %get-tuple-element.10), channel_id=1, source_target_pairs={{0,1},{1,2},{2,3},{3,4},{4,5},{5,6},{6,7},{7,8},{8,9},{9,10},{10,1... | collective-permute-start | bytes 3145736 | tf_op jit(solution)/shard_map/ppermute | solution.py:22
  26.4 1.9 %collective-permute-start.1 = (f32[2048,128]{1,0:T(8,128)}, f32[2048,128]{1,0:T(8,128)S(1)}, u32[]{:S(2)}, u32[]{:S(2)}) collective-permute-start(f32[2048,128]{1,0:T(8,128)} %get-tuple-element.11), channel_id=1, source_target_pairs={{1,0},{2,1},{3,2},{4,3},{5,4},{6,5},{7,6},{8,7},{9,8},{10,9},{11,1... | collective-permute-start | bytes 3145736 | tf_op jit(solution)/shard_map/ppermute | solution.py:22
  28.5 0.7 fusion.38
  29.2 2.6 %fusion.36 = (s32[]{:T(128)}, s32[]{:T(128)}) fusion(s32[14]{0:T(128)S(1)} %slice.34, s32[1]{0:T(128)} %get-tuple-element.20, s32[1]{0:T(128)} %get-tuple-element.21, s32[]{:T(128)S(6)} %axis_index.12, s32[1]{0:T(128)} %get-tuple-element.19, s32[15]{0:T(128)S(1)} %slice.35), kind=kLoop, calls=%fused_computation.79 | loop fusion | flops 126 | bytes 140 | tf_op jit(solution)/shard_map/reduce_sum | solution.py:56
  33.0 16.7 %collective-permute-done = f32[2048,128]{1,0:T(8,128)S(1)} collective-permute-done((f32[2048,128]{1,0:T(8,128)}, f32[2048,128]{1,0:T(8,128)S(1)}, u32[]{:S(2)}, u32[]{:S(2)}) %collective-permute-start) | collective-permute-done | bytes 1048608 | tf_op jit(solution)/shard_map/ppermute | solution.py:22
  49.7 1.8 %collective-permute-done.1 = f32[2048,128]{1,0:T(8,128)S(1)} collective-permute-done((f32[2048,128]{1,0:T(8,128)}, f32[2048,128]{1,0:T(8,128)S(1)}, u32[]{:S(2)}, u32[]{:S(2)}) %collective-permute-start.1) | collective-permute-done | bytes 1048608 | tf_op jit(solution)/shard_map/ppermute | solution.py:22
  51.5 1.0 %copy-done.2 = f32[2048,128]{1,0:T(8,128)} copy-done((f32[2048,128]{1,0:T(8,128)}, f32[2048,128]{1,0:T(8,128)S(1)}, u32[]{:S(2)}) %copy-start.2) | copy-done | bytes 1048600
  52.5 1.7 %broadcast_select_fusion.7 = (f32[2048,128]{1,0:T(8,128)S(1)}, f32[2048,128]{1,0:T(8,128)S(1)}) fusion(pred[]{:T(512)S(6)} %lt.6, f32[2048,128]{1,0:T(8,128)S(1)} %get-tuple-element.12, f32[2048,128]{1,0:T(8,128)} %copy-done.1, pred[]{:T(512)S(6)} %eq.72, f32[2048,128]{1,0:T(8,128)} %copy-done.2, pred[]{:T(512)S(6)} %eq.76), kind=kLoop, calls=%fused_computation.50 | loop fusion | flops 1048576 | bytes 5242883 | tf_op jit(solution)/shard_map/jit(_where)/select_n | solution.py:59
  54.2 1.8 %fusion.47 = f32[128,128]{1,0:T(8,128)S(1)} fusion(f32[2048,128]{1,0:T(8,128)S(1)} %get-tuple-element.13, f32[2048,128]{1,0:T(8,128)S(1)} %get-tuple-element.14), kind=kOutput, calls=%fused_computation.94 | convolution fusion | flops 402653184 | bytes 2162688 | tf_op jit(solution)/shard_map/dot_general | solution.py:45
  56.0 4.0 %all-gather.1 = f32[256,128]{1,0:T(8,128)S(1)} all-gather(f32[128,128]{1,0:T(8,128)S(1)} %fusion.47), channel_id=3, replica_groups=mesh['row'=2,'pair'=16] {'row'}, dimensions={0}, use_global_device_ids=true | all-gather | bytes 196608 | tf_op jit(solution)/shard_map/all_gather | solution.py:13
  60.0 0.6 multiply_reduce_fusion
  61.3 0.3 fusion.3
  62.8 0.3 fusion.7
  64.3 1.0 %convolution_subtract_fusion = f32[2048,128]{1,0:T(8,128)S(1)} fusion(f32[2048,128]{1,0:T(8,128)S(1)} %get-tuple-element.14, f32[2048,128]{1,0:T(8,128)S(1)} %get-tuple-element.13, f32[128,128]{1,0:T(8,128)S(1)} %reduce_sum.78, f32[]{:T(128)S(6)} %div.35), kind=kOutput, calls=%fused_computation | convolution fusion | flops 402931712 | bytes 3211268 | tf_op jit(solution)/shard_map/dot_general | solution.py:69
  65.3 1.0 %convolution_add_fusion = f32[2048,128]{1,0:T(8,128)S(1)} fusion(f32[2048,128]{1,0:T(8,128)S(1)} %get-tuple-element.13, f32[2048,128]{1,0:T(8,128)S(1)} %get-tuple-element.14, f32[128,128]{1,0:T(8,128)S(1)} %reduce_sum.78, f32[]{:T(128)S(6)} %div.35), kind=kOutput, calls=%fused_computation.1 | convolution fusion | flops 402931712 | bytes 3211268 | tf_op jit(solution)/shard_map/dot_general | solution.py:66
  67.1 1.0 %fusion.51 = f32[2048,128]{1,0:T(8,128)S(1)} fusion(f32[2048,128]{1,0:T(8,128)S(1)} %convolution_add_fusion, f32[128,128]{1,0:T(8,128)S(1)} %convolution_multiply_fusion.4), kind=kOutput, calls=%fused_computation.98 | convolution fusion | flops 402653184 | bytes 2162688 | tf_op jit(solution)/shard_map/dot_general | solution.py:65
  68.1 1.0 %broadcast_select_fusion.9 = (f32[2048,128]{1,0:T(8,128)S(1)}, f32[2048,128]{1,0:T(8,128)S(1)}, f32[2048,128]{1,0:T(8,128)S(1)}) fusion(pred[]{:T(512)S(6)} %eq.72, f32[2048,128]{1,0:T(8,128)S(1)} %fusion.51, pred[]{:T(512)S(6)} %lt.6, f32[2048,128]{1,0:T(8,128)S(1)} %convolution_subtract_fusion, f32[128,128]{1,0:T(8,128)S(1)} %convolution_multiply_fusion), kind=kOutput, calls=%fused_computation.52 | convolution fusion | flops 403439616 | bytes 5308418 | tf_op jit(solution)/shard_map/dot_general | solution.py:68
  69.1 4.6 %collective-permute-start.2 = (f32[2048,128]{1,0:T(8,128)S(1)}, f32[2048,128]{1,0:T(8,128)S(1)}, u32[]{:S(2)}, u32[]{:S(2)}) collective-permute-start(f32[2048,128]{1,0:T(8,128)S(1)} %get-tuple-element.7), channel_id=1, source_target_pairs={{0,1},{1,2},{2,3},{3,4},{4,5},{5,6},{6,7},{7,8},{8,9},{9,10},{10,1... | collective-permute-start | bytes 3145736 | tf_op jit(solution)/shard_map/ppermute | solution.py:22
  73.8 1.9 %collective-permute-start.3 = (f32[2048,128]{1,0:T(8,128)S(1)}, f32[2048,128]{1,0:T(8,128)S(1)}, u32[]{:S(2)}, u32[]{:S(2)}) collective-permute-start(f32[2048,128]{1,0:T(8,128)S(1)} %get-tuple-element.8), channel_id=1, source_target_pairs={{1,0},{2,1},{3,2},{4,3},{5,4},{6,5},{7,6},{8,7},{9,8},{10,9},{11,1... | collective-permute-start | bytes 3145736 | tf_op jit(solution)/shard_map/ppermute | solution.py:22
  75.7 21.0 %collective-permute-done.2 = f32[2048,128]{1,0:T(8,128)S(1)} collective-permute-done((f32[2048,128]{1,0:T(8,128)S(1)}, f32[2048,128]{1,0:T(8,128)S(1)}, u32[]{:S(2)}, u32[]{:S(2)}) %collective-permute-start.2) | collective-permute-done | bytes 1048608 | tf_op jit(solution)/shard_map/ppermute | solution.py:22
  96.9 1.5 %pad_maximum_fusion = f32[2048,256]{1,0:T(8,128)} fusion(f32[2048,128]{1,0:T(8,128)S(1)} %get-tuple-element.18, f32[2048,128]{1,0:T(8,128)S(1)} %get-tuple-element.17), kind=kLoop, calls=%fused_computation.4 | loop fusion | flops 524288 | bytes 4194304 | tf_op jit(solution)/shard_map/concatenate | solution.py:92
  (45 shorter events, 6.7 us)
Async XLA Ops:
  17.4 1.8 %copy-start = (f32[2048,128]{1,0:T(8,128)S(1)}, f32[2048,128]{1,0:T(8,128)}, u32[]{:S(2)}) copy-start(f32[2048,128]{1,0:T(8,128)} %convolution_subtract_fusion.1) | copy-start | bytes 3145732
  19.3 9.1 %copy-start.3 = (s32[32]{0:T(128)S(1)}, s32[32]{0:T(128)}, u32[]{:S(2)}) copy-start(s32[32]{0:T(128)} %param.3) | copy-start | bytes 388
  21.6 28.1 %collective-permute-start = (f32[2048,128]{1,0:T(8,128)}, f32[2048,128]{1,0:T(8,128)S(1)}, u32[]{:S(2)}, u32[]{:S(2)}) collective-permute-start(f32[2048,128]{1,0:T(8,128)} %get-tuple-element.10), channel_id=1, source_target_pairs={{0,1},{1,2},{2,3},{3,4},{4,5},{5,6},{6,7},{7,8},{8,9},{9,10},{10,1... | collective-permute-start | bytes 3145736 | tf_op jit(solution)/shard_map/ppermute | solution.py:22
  26.4 25.1 %collective-permute-start.1 = (f32[2048,128]{1,0:T(8,128)}, f32[2048,128]{1,0:T(8,128)S(1)}, u32[]{:S(2)}, u32[]{:S(2)}) collective-permute-start(f32[2048,128]{1,0:T(8,128)} %get-tuple-element.11), channel_id=1, source_target_pairs={{1,0},{2,1},{3,2},{4,3},{5,4},{6,5},{7,6},{8,7},{9,8},{10,9},{11,1... | collective-permute-start | bytes 3145736 | tf_op jit(solution)/shard_map/ppermute | solution.py:22
  49.7 1.8 %copy-start.1 = (f32[2048,128]{1,0:T(8,128)}, f32[2048,128]{1,0:T(8,128)S(1)}, u32[]{:S(2)}) copy-start(f32[2048,128]{1,0:T(8,128)S(1)} %collective-permute-done) | copy-start | bytes 3145732
  51.5 1.0 %copy-start.2 = (f32[2048,128]{1,0:T(8,128)}, f32[2048,128]{1,0:T(8,128)S(1)}, u32[]{:S(2)}) copy-start(f32[2048,128]{1,0:T(8,128)S(1)} %collective-permute-done.1) | copy-start | bytes 3145732
  69.1 27.6 %collective-permute-start.2 = (f32[2048,128]{1,0:T(8,128)S(1)}, f32[2048,128]{1,0:T(8,128)S(1)}, u32[]{:S(2)}, u32[]{:S(2)}) collective-permute-start(f32[2048,128]{1,0:T(8,128)S(1)} %get-tuple-element.7), channel_id=1, source_target_pairs={{0,1},{1,2},{2,3},{3,4},{4,5},{5,6},{6,7},{7,8},{8,9},{9,10},{10,1... | collective-permute-start | bytes 3145736 | tf_op jit(solution)/shard_map/ppermute | solution.py:22
  73.8 23.0 %collective-permute-start.3 = (f32[2048,128]{1,0:T(8,128)S(1)}, f32[2048,128]{1,0:T(8,128)S(1)}, u32[]{:S(2)}, u32[]{:S(2)}) collective-permute-start(f32[2048,128]{1,0:T(8,128)S(1)} %get-tuple-element.8), channel_id=1, source_target_pairs={{1,0},{2,1},{3,2},{4,3},{5,4},{6,5},{7,6},{8,7},{9,8},{10,9},{11,1... | collective-permute-start | bytes 3145736 | tf_op jit(solution)/shard_map/ppermute | solution.py:22
